TPU v7x, 32 devices: a whole 2x2x4 slice. The times are simulated.
32 devices in a mesh: groups: 2 (over y), ctx: 4 (over z), exp: 2 (over x), tp: 2 (over core).
Axes of the slice: x: 2, y: 2, z: 4, core: 2. Of those that a mesh axis runs over, the one named last changes fastest.
Arguments:
- queries: bfloat16 [4, 512, 20, 128], P(('groups', 'exp'), 'ctx', 'tp'), parts along dimension 0, may hold values from -9 to 9
- key_states: bfloat16 [4, 512, 4, 128], P(('groups', 'exp'), 'ctx', 'tp'), parts along dimension 0, may hold values from -9 to 9
- values: bfloat16 [4, 512, 4, 128], P(('groups', 'exp'), 'ctx', 'tp'), parts along dimension 0, may hold values from -6 to 6
- doc_ids: int32 [4, 512], P(('groups', 'exp'), 'ctx'), parts along dimension 0, may hold values from 0 to 3, never falling along the last dimension, each value on 1 to 256 neighbouring positions
- residual: bfloat16 [4, 512, 5120], P(('groups', 'exp'), ('ctx', 'tp')), parts along dimension 0, may hold values from -6 to 6
- out_proj: bfloat16 [2560, 5120], P('tp', 'ctx'), may hold values from -0.125 to 0.125
- norm_gain: bfloat16 [5120], replicated, may hold values from 0.5 to 1.5
- router: bfloat16 [5120, 64], P(None, 'exp'), may hold values from -0.078125 to 0.078125
- expert_ids: int32 [4, 512, 1], P(('groups', 'exp'), ('ctx', 'tp')), parts along dimension 0, may hold values from 0 to 63; in each aligned block of 64 rows (0 to 63, 64 to 127, ..., all dimensions but the last counted through in order) at most 2 rows name the same one
- keep_counts: int32 [128], P('groups'), parts along dimension 0, may hold values from 1 to 2
Outputs:
- expert_inputs: bfloat16 [32, 64, 2, 5120], P(('groups', 'ctx', 'tp'), 'exp'), parts along dimension 0
There are 2 independent parts, one for each index of `groups`. A program takes and returns all parts, laid end to end along the dimension named above; an argument that names none is the same for every part. Nothing has to cross between parts.
Inputs may be any that keep to these rules, and one draw needn't show every extreme that they name: `doc_ids`: doc ids never fall along a request; a document holds at most 256 tokens, and some document holds exactly that many. `expert_ids`: in each aligned block of 64 tokens (the rows of one device) no expert is named more than 2 times, and in some blocks one expert is named exactly 2 times.
All inputs are finite; a program needn't handle non-finite values.
Results may differ from a plain program's by a relative error of at most 0.013.
Values may be sent and summed in bfloat16 or wider, within the bound.
A program may use at most 64 MiB of HBM per device.

v0:
```python
import math
import jax
import jax.numpy as jnp
from jax import lax
from jax.sharding import PartitionSpec as P

CAP = 2
EPSILON = 1e-05


def on_device(
    queries,
    key_states,
    values,
    doc_ids,
    residual,
    out_proj,
    norm_gain,
    router,
    expert_ids,
    keep_counts,
):
    tokens_here = queries.shape[1]
    heads_here = queries.shape[2]
    head_size = queries.shape[3]
    groups_here = key_states.shape[2]
    mixing_ratio = heads_here // groups_here
    ctx_count = lax.axis_size("ctx")
    pair_count = lax.axis_size("tp")
    part_rows = tokens_here // pair_count
    first_token = lax.axis_index("ctx") * tokens_here
    scale = 1.0 / math.sqrt(head_size)
    query_rows = (
        queries[0].reshape(tokens_here, groups_here, mixing_ratio, head_size).transpose(1, 0, 2, 3)
    )
    query_rows = query_rows.reshape(groups_here, tokens_here * mixing_ratio, head_size)
    query_place = (
        first_token
        + lax.broadcasted_iota(jnp.int32, (tokens_here * mixing_ratio,), 0) // mixing_ratio
    )
    query_docs = jnp.repeat(doc_ids[0], mixing_ratio)

    def update(running, key_block, value_block, doc_block, key_first):
        highest, totals, accum = running
        scores = (
            jnp.einsum("gqd,kgd->gqk", query_rows, key_block, preferred_element_type=jnp.float32)
            * scale
        )
        key_place = key_first + lax.broadcasted_iota(jnp.int32, (key_block.shape[0],), 0)
        allowed = (key_place[None, :] <= query_place[:, None]) & (
            doc_block[None, :] == query_docs[:, None]
        )
        masked = jnp.where(allowed[None], scores, -1e30)
        new_highest = jnp.maximum(highest, jnp.max(masked, axis=2))
        weights = jnp.where(allowed[None], jnp.exp(scores - new_highest[..., None]), 0.0)
        factor = jnp.exp(highest - new_highest)
        totals = totals * factor + jnp.sum(weights, axis=2)
        accum = accum * factor[..., None] + jnp.einsum(
            "gqk,kgd->gqd",
            weights.astype(jnp.bfloat16),
            value_block,
            preferred_element_type=jnp.float32,
        )
        return (new_highest, totals, accum)

    start_state = (
        jnp.full((groups_here, tokens_here * mixing_ratio), -1e30, jnp.float32),
        jnp.zeros((groups_here, tokens_here * mixing_ratio), jnp.float32),
        jnp.zeros((groups_here, tokens_here * mixing_ratio, head_size), jnp.float32),
    )
    key_piece = lax.all_gather(key_states, "ctx", axis=1, tiled=True)
    value_piece = lax.all_gather(values, "ctx", axis=1, tiled=True)
    doc_piece = lax.all_gather(doc_ids, "ctx", axis=1, tiled=True)
    piece_rows = key_piece.shape[1]
    block_rows = math.gcd(piece_rows, 512)

    def step(block_number, inner):
        block_offset = block_number * block_rows
        key_block = lax.dynamic_slice_in_dim(key_piece[0], block_offset, block_rows, 0)
        value_block = lax.dynamic_slice_in_dim(value_piece[0], block_offset, block_rows, 0)
        doc_block = lax.dynamic_slice_in_dim(doc_piece[0], block_offset, block_rows, 0)
        return update(inner, key_block, value_block, doc_block, block_offset)

    highest, totals, accum = lax.fori_loop(0, piece_rows // block_rows, step, start_state)
    blended_output = (accum / totals[..., None]).astype(jnp.bfloat16)
    blended_output = blended_output.reshape(
        groups_here, tokens_here, mixing_ratio, head_size
    ).transpose(1, 0, 2, 3)
    attn_rows = blended_output.reshape(pair_count, part_rows, heads_here * head_size)
    columns = out_proj.shape[1]
    gathered = lax.all_gather(attn_rows, "ctx", axis=1, tiled=True)
    gathered = gathered.reshape(pair_count * ctx_count * part_rows, heads_here * head_size)
    own_columns = lax.psum_scatter(
        jnp.dot(gathered, out_proj, preferred_element_type=jnp.float32).astype(jnp.bfloat16),
        "tp",
        scatter_dimension=0,
        tiled=True,
    ).astype(jnp.float32)
    own_columns = own_columns.reshape(ctx_count, part_rows, columns)
    projected = (
        lax.all_to_all(
            own_columns.astype(jnp.bfloat16), "ctx", split_axis=0, concat_axis=2, tiled=True
        )
        .astype(own_columns.dtype)
        .reshape(part_rows, columns * ctx_count)
    )
    hidden = residual[0].astype(jnp.float32) + projected
    power = jnp.mean(hidden * hidden, axis=1, keepdims=True)
    normed = (hidden * lax.rsqrt(power + EPSILON) * norm_gain.astype(jnp.float32)).astype(
        jnp.bfloat16
    )
    expert_count = keep_counts.shape[0]
    chosen = expert_ids[0, :, 0]
    onehot = (
        chosen[:, None] == lax.broadcasted_iota(jnp.int32, (part_rows, expert_count), 1)
    ).astype(jnp.float32)
    lower = (
        lax.broadcasted_iota(jnp.int32, (part_rows, part_rows), 0)
        > lax.broadcasted_iota(jnp.int32, (part_rows, part_rows), 1)
    ).astype(jnp.float32)
    earlier = jnp.dot(lower, onehot, preferred_element_type=jnp.float32)
    ranking = jnp.sum(onehot * earlier, axis=1)
    limits = jnp.sum(onehot * keep_counts.astype(jnp.float32)[None, :], axis=1)
    kept = ranking < limits
    target = chosen.astype(jnp.float32) * CAP + ranking
    slot_iota = lax.broadcasted_iota(jnp.int32, (expert_count * CAP, part_rows), 0).astype(
        jnp.float32
    )
    table = (slot_iota == target[None, :]) & kept[None, :]
    outgoing = jnp.dot(
        table.astype(jnp.bfloat16), normed, preferred_element_type=jnp.float32
    ).astype(jnp.bfloat16)
    exp_count = lax.axis_size("exp")
    outgoing = outgoing.reshape(exp_count, expert_count // exp_count, CAP, normed.shape[1])
    arrived = lax.all_to_all(outgoing, "exp", split_axis=0, concat_axis=0, tiled=True)
    logits = jnp.einsum("secd,de->sec", arrived, router, preferred_element_type=jnp.float32)
    return (arrived.astype(jnp.float32) * jax.nn.sigmoid(logits)[..., None]).astype(jnp.bfloat16)


def solution(mesh):
    placed = (
        P(("groups", "exp"), "ctx", "tp", None),
        P(("groups", "exp"), "ctx", "tp", None),
        P(("groups", "exp"), "ctx", "tp", None),
        P(("groups", "exp"), "ctx"),
        P(("groups", "exp"), ("ctx", "tp"), None),
        P("tp", "ctx"),
        P(),
        P(None, "exp"),
        P(("groups", "exp"), ("ctx", "tp"), None),
        P("groups"),
    )
    return jax.shard_map(
        on_device,
        mesh=mesh,
        in_specs=placed,
        out_specs=P(("groups", "ctx", "tp"), "exp", None, None),
        check_vma=False,
    )
```

profile of v0, /device:TPU:0, one launch (start us, length us, event | category | flops | bytes accessed | tf_op | source)
XLA Modules:
  0.0 172.3 jit_solution(3476322581073212627)
XLA Ops:
  6.5 12.9 %all_gather.14 = s32[1,512]{1,0:T(1,128)S(1)} all-gather(s32[1,128]{1,0:T(1,128)} %param.13), channel_id=1, replica_groups=mesh['groups'=2,'ctx'=4,'exp'=2,'tp'=2] {'ctx'}, dimensions={1}, use_global_device_ids=true | all-gather | bytes 2560 | tf_op jit(solution)/shard_map/all_gather | solution.py:73
  19.5 0.7 broadcast_in_dim.55
  20.2 0.2 eq.47
  20.4 0.9 copy.17
  21.3 13.9 %all_gather.16 = bf16[1,512,2,128]{3,1,2,0:T(8,128)(2,1)S(1)} all-gather(bf16[1,128,2,128]{3,1,2,0:T(8,128)(2,1)S(1)} %copy.17), channel_id=1, replica_groups=mesh['groups'=2,'ctx'=4,'exp'=2,'tp'=2] {'ctx'}, dimensions={1}, use_global_device_ids=true | all-gather | bytes 327680 | tf_op jit(solution)/shard_map/all_gather | solution.py:71
  35.2 1.3 copy.16
  36.5 0.3 fusion.7
  36.8 0.7 select_reduce_fusion
  37.5 0.6 fusion
  38.1 0.2 copy-done.2
  38.3 14.1 %all_gather.17 = bf16[1,512,2,128]{3,1,2,0:T(8,128)(2,1)S(1)} all-gather(bf16[1,128,2,128]{3,1,2,0:T(8,128)(2,1)S(1)} %copy.19), channel_id=1, replica_groups=mesh['groups'=2,'ctx'=4,'exp'=2,'tp'=2] {'ctx'}, dimensions={1}, use_global_device_ids=true | all-gather | bytes 327680 | tf_op jit(solution)/shard_map/all_gather | solution.py:72
  52.5 1.2 fusion.18
  53.7 0.3 copy.21
  54.0 0.9 copy.22
  54.9 2.2 %reshape.135 = bf16[2,64,1280]{2,1,0:T(8,128)(2,1)} reshape(bf16[128,2,5,128]{3,2,1,0:T(8,128)(2,1)} %copy.22) | data formatting | bytes 655360 | tf_op jit(solution)/shard_map/reshape | solution.py:89
  57.1 30.9 %all-gather.2.cloned.1.call-done = bf16[2,256,1280]{2,1,0:T(8,128)(2,1)} async-done(((bf16[2,64,1280]{2,1,0:T(8,128)(2,1)}), bf16[2,256,1280]{2,1,0:T(8,128)(2,1)}) %all-gather.2.cloned.1.call-update) | async-done | bytes 1310736 | tf_op jit(solution)/shard_map/all_gather | solution.py:91
  88.1 4.2 %convolution_convert_fusion.1 = bf16[512,1280]{1,0:T(8,128)(2,1)} fusion(bf16[512,1280]{1,0:T(8,128)(2,1)} %bitcast.62, bf16[1280,1280]{1,0:T(8,128)(2,1)S(1)} %copy-done), kind=kOutput, calls=%fused_computation.1 | convolution fusion | flops 1678376960 | bytes 5898240 | tf_op jit(solution)/shard_map/dot_general | solution.py:94
  92.3 7.9 %reduce-scatter.2.cloned.1.call-done = bf16[256,1280]{1,0:T(8,128)(2,1)} async-done(((bf16[512,1280]{1,0:T(8,128)(2,1)}), bf16[256,1280]{1,0:T(8,128)(2,1)}) %reduce-scatter.2.cloned.1.call-update) | async-done | bytes 655376 | tf_op jit(solution)/shard_map/reduce_scatter | solution.py:93
  100.3 5.0 %all-to-all-start = ((bf16[4,64,1280]{2,1,0:T(8,128)(2,1)}), bf16[4,64,1280]{2,1,0:T(8,128)(2,1)}, u32[]{:S(2)}, u32[]{:S(2)}) async-start(bf16[4,64,1280]{2,1,0:T(8,128)(2,1)} %bitcast.55), calls=%async_computation.1 | async-start | bytes 1310720 | tf_op jit(solution)/shard_map/all_to_all | solution.py:101
  105.3 0.2 fusion.14
  105.4 0.1 select_reduce_fusion.1
  105.6 17.4 %all-to-all-done = bf16[4,64,1280]{2,1,0:T(8,128)(2,1)} async-done(((bf16[4,64,1280]{2,1,0:T(8,128)(2,1)}), bf16[4,64,1280]{2,1,0:T(8,128)(2,1)}, u32[]{:S(2)}, u32[]{:S(2)}) %all-to-all-start) | async-done | bytes 655392 | tf_op jit(solution)/shard_map/all_to_all | solution.py:101
  123.0 1.2 convert_bitcast_fusion
  124.2 0.8 copy.23
  125.0 0.2 copy.28
  125.3 0.8 copy-done.1
  126.1 0.3 multiply_reduce_fusion
  126.4 1.6 convolution_convert_fusion
  128.0 3.9 %reshape.137 = bf16[2,32,2,5120]{3,2,1,0:T(2,128)(2,1)} reshape(bf16[128,5120]{1,0:T(8,128)(2,1)} %convolution_convert_fusion) | data formatting | bytes 2621440 | tf_op jit(solution)/shard_map/reshape | solution.py:134
  131.9 19.7 %all_to_all.14 = bf16[2,32,2,5120]{3,2,1,0:T(2,128)(2,1)S(1)} all-to-all(bf16[2,32,2,5120]{3,2,1,0:T(2,128)(2,1)} %reshape.137), channel_id=1, replica_groups=mesh['groups'=2,'ctx'=4,'exp'=2,'tp'=2] {'exp'}, dimensions={0} | all-to-all | bytes 2621440 | tf_op jit(solution)/shard_map/all_to_all | solution.py:135
  151.6 11.5 %fusion.9 = f32[32,1,2,2]{3,1,2,0:T(1,128)S(1)} fusion(bf16[2,32,2,5120]{3,2,1,0:T(2,128)(2,1)S(1)} %all_to_all.14, bf16[5120,32,1,1]{0,1,2,3:T(8,128)(2,1)S(1)} %bitcast.63), kind=kOutput, calls=%fused_computation.18 | convolution fusion | flops 1310720 | bytes 1638912 | tf_op jit(solution)/shard_map/secd,de->sec/dot_general | solution.py:136
  163.2 2.2 %multiply_convert_fusion = bf16[2,32,2,5120]{3,2,1,0:T(2,128)(2,1)} fusion(bf16[2,32,2,5120]{3,2,1,0:T(2,128)(2,1)S(1)} %all_to_all.14, f32[2,32,2]{2,1,0:T(8,128)S(1)} %fusion.34), kind=kLoop, calls=%fused_computation.2 | loop fusion | flops 1966080 | bytes 2621952 | tf_op jit(solution)/shard_map/convert_element_type | solution.py:137
  (26 shorter events, 0.2 us)
Async XLA Ops:
  6.5 81.5 %copy-start = (bf16[1280,1280]{1,0:T(8,128)(2,1)S(1)}, bf16[1280,1280]{1,0:T(8,128)(2,1)}, u32[]{:S(2)}) copy-start(bf16[1280,1280]{1,0:T(8,128)(2,1)} %param.15) | copy-start | bytes 9830404
  6.5 81.5 %all-gather.2.cloned.1.call-start = ((), (), s32[]{:S(2)}) async-start(), calls=%async_computation.3 | async-start | bytes 1638400 | tf_op jit(solution)/shard_map/all_gather | solution.py:91
  37.5 0.8 copy-start.2
  57.1 43.2 %reduce-scatter.2.cloned.1.call-start = ((), (), s32[]{:S(2)}) async-start(), calls=%async_computation.4 | async-start | bytes 1966080 | tf_op jit(solution)/shard_map/reduce_scatter | solution.py:93
  92.3 13.0 %copy-start.6 = (s32[64]{0:T(128)S(1)}, s32[64]{0:T(128)}, u32[]{:S(2)}) copy-start(s32[64]{0:T(128)} %param.19) | copy-start | bytes 772
  92.3 13.0 %copy-start.3 = (bf16[5120]{0:T(1024)(128)(2,1)S(1)}, bf16[5120]{0:T(1024)(128)(2,1)}, u32[]{:S(2)}) copy-start(bf16[5120]{0:T(1024)(128)(2,1)} %param.16) | copy-start | bytes 30724
  92.3 13.0 %copy-start.4 = (s32[1,64,1]{1,2,0:T(1,128)S(1)}, s32[1,64,1]{1,2,0:T(1,128)}, u32[]{:S(2)}) copy-start(s32[1,64,1]{1,2,0:T(1,128)} %param.18) | copy-start | bytes 772
  100.3 22.7 %all-to-all-start = ((bf16[4,64,1280]{2,1,0:T(8,128)(2,1)}), bf16[4,64,1280]{2,1,0:T(8,128)(2,1)}, u32[]{:S(2)}, u32[]{:S(2)}) async-start(bf16[4,64,1280]{2,1,0:T(8,128)(2,1)} %bitcast.55), calls=%async_computation.1 | async-start | bytes 1310720 | tf_op jit(solution)/shard_map/all_to_all | solution.py:101
  125.0 1.1 copy-start.1
  131.9 19.7 %copy-start.5 = (bf16[5120,32]{0,1:T(8,128)(2,1)S(1)}, bf16[5120,32]{0,1:T(8,128)(2,1)}, u32[]{:S(2)}) copy-start(bf16[5120,32]{0,1:T(8,128)(2,1)} %param.17) | copy-start | bytes 983044
Sparse Core Ops, SparseCore 0:
  57.2 30.8 all-gather.1
  92.4 7.7 reduce-scatter.1
where the time goes:
time: 173 us; the launch traced here: 172 us
  blocking collectives  60.6 us (35%)
  waiting for transfers between devices  56.3 us (33%)
  matrix products  19.5 us (11%)
  between operations  13.6 us (8%)
  local copies, waits for them, and re-layouts  12.5 us (7%)
  starting transfers between devices  5.02 us (3%)
  other arithmetic  4.83 us (3%)
    all_gather x1, waiting for transfers between devices, on_device(): gathered = lax.all_gather(attn_rows, 'ctx', axis=1, tiled=True)  30.9 us
    all_to_all x1, blocking collectives, on_device(): lax.all_to_all(outgoing, 'exp', split_axis=0, concat_axis=0, tiled=True)  19.7 us
    all_to_all x1, waiting for transfers between devices, on_device(): lax.all_to_all(own_columns.astype(jnp.bfloat16), 'ctx', split_axis=0, con...  17.4 us
    all_gather x1, blocking collectives, on_device(): value_piece = lax.all_gather(values, 'ctx', axis=1, tiled=True)  14.1 us
    all_gather x1, blocking collectives, on_device(): key_piece = lax.all_gather(key_states, 'ctx', axis=1, tiled=True)  13.9 us
    all_gather x1, blocking collectives, on_device(): doc_piece = lax.all_gather(doc_ids, 'ctx', axis=1, tiled=True)  12.9 us
    dot_general x1, matrix products, on_device(): jnp.einsum('secd,de->sec', arrived, router, preferred_element_type=jnp.fl...  11.5 us
    reduce_scatter x1, waiting for transfers between devices, on_device(): lax.psum_scatter(jnp.dot(gathered, out_proj, preferred_element_type=jnp.f...  7.95 us
  transfers between devices with their start and end apart: 3, of which 3 were waited for; matrix products, arithmetic and copies ran while one was open for 0% of the time, Pallas kernels for 0%

commit v1 on v0

--- a/solution.py
+++ b/solution.py
@@ -68,7 +68,15 @@
         jnp.zeros((groups_here, tokens_here * mixing_ratio), jnp.float32),
         jnp.zeros((groups_here, tokens_here * mixing_ratio, head_size), jnp.float32),
     )
-    key_piece = lax.all_gather(key_states, "ctx", axis=1, tiled=True)
+    parts_n = lax.psum(1, "ctx")
+    carry_in = sorted(((dev_j, (dev_j + 1) % parts_n) for dev_j in range(parts_n)))
+    vec_out = key_states
+    blocks_here = [vec_out]
+    for t in range(1, parts_n):
+        vec_out = lax.ppermute(vec_out, "ctx", carry_in)
+        blocks_here.insert(0, vec_out)
+    local_part = jnp.concatenate(blocks_here, axis=1)
+    key_piece = jnp.roll(local_part, (lax.axis_index("ctx") + 1) * key_states.shape[1], axis=1)
     value_piece = lax.all_gather(values, "ctx", axis=1, tiled=True)
     doc_piece = lax.all_gather(doc_ids, "ctx", axis=1, tiled=True)
     piece_rows = key_piece.shape[1]

time: 173 us -> 166 us (0.960)
  blocking collectives: 60.6 us -> 44 us
  waiting for transfers between devices: 56.3 us -> 61.4 us
  starting transfers between devices: 5.02 us -> 8.16 us
    all_gather x1 -> x0, blocking collectives: 13.9 us -> none  [on_device(): key_piece = lax.all_gather(key_states, 'ctx', axis=1, tiled=True)]
    ppermute x0 -> x3, starting transfers between devices: none -> 3.14 us  [on_device(): vec_out = lax.ppermute(vec_out, 'ctx', carry_in)]
    all_gather x1, waiting for transfers between devices: 30.9 us -> 33.9 us  [on_device(): gathered = lax.all_gather(attn_rows, 'ctx', axis=1, tiled=True)]
    all_gather x1, blocking collectives: 12.9 us -> 9.89 us  [on_device(): doc_piece = lax.all_gather(doc_ids, 'ctx', axis=1, tiled=True)]
    ppermute x0 -> x3, waiting for transfers between devices: none -> 2.07 us  [on_device(): vec_out = lax.ppermute(vec_out, 'ctx', carry_in)]
  transfers between devices with their start and end apart: 3 -> 6, of which waited for: 3 -> 4; matrix products, arithmetic and copies ran while one was open for 0% -> 3% of each run, Pallas kernels for 0% -> 0%
where the time goes in v1:
time: 166 us
  waiting for transfers between devices  61.4 us (37%)
  blocking collectives  44 us (27%)
  matrix products  19.5 us (12%)
  local copies, waits for them, and re-layouts  13.6 us (8%)
  between operations  13.6 us (8%)
  starting transfers between devices  8.16 us (5%)
  other arithmetic  5.56 us (3%)
    all_gather x1, waiting for transfers between devices, on_device(): gathered = lax.all_gather(attn_rows, 'ctx', axis=1, tiled=True)  33.9 us
    all_to_all x1, blocking collectives, on_device(): lax.all_to_all(outgoing, 'exp', split_axis=0, concat_axis=0, tiled=True)  19.7 us
    all_to_all x1, waiting for transfers between devices, on_device(): lax.all_to_all(own_columns.astype(jnp.bfloat16), 'ctx', split_axis=0, con...  17.4 us
    all_gather x1, blocking collectives, on_device(): value_piece = lax.all_gather(values, 'ctx', axis=1, tiled=True)  14.4 us
    dot_general x1, matrix products, on_device(): jnp.einsum('secd,de->sec', arrived, router, preferred_element_type=jnp.fl...  11.5 us
    all_gather x1, blocking collectives, on_device(): doc_piece = lax.all_gather(doc_ids, 'ctx', axis=1, tiled=True)  9.89 us
    reduce_scatter x1, waiting for transfers between devices, on_device(): lax.psum_scatter(jnp.dot(gathered, out_proj, preferred_element_type=jnp.f...  7.95 us
    all_to_all x1, starting transfers between devices, on_device(): lax.all_to_all(own_columns.astype(jnp.bfloat16), 'ctx', split_axis=0, con...  4.98 us
  transfers between devices with their start and end apart: 6, of which 4 were waited for; matrix products, arithmetic and copies ran while one was open for 3% of the time, Pallas kernels for 0%

profile of v1, /device:TPU:0, one launch (start us, length us, event | category | flops | bytes accessed | tf_op | source)
XLA Modules:
  0.0 165.8 jit_solution(3278054453467832915)
XLA Ops:
  6.5 3.1 %collective-permute-start = (bf16[1,128,2,128]{3,2,1,0:T(2,128)(2,1)}, bf16[1,128,2,128]{3,2,1,0:T(2,128)(2,1)S(1)}, u32[]{:S(2)}, u32[]{:S(2)}) collective-permute-start(bf16[1,128,2,128]{3,2,1,0:T(2,128)(2,1)} %param.11), channel_id=1, source_target_pairs={{0,4},{4,8},{8,12},{12,0},{1,5},{5,9},{9,13},{13,1},{2,6},{6,10},{... | collective-permute-start | bytes 196616 | tf_op jit(solution)/shard_map/ppermute | solution.py:76
  9.6 9.9 %all_gather.11 = s32[1,512]{1,0:T(1,128)S(1)} all-gather(s32[1,128]{1,0:T(1,128)} %param.13), channel_id=1, replica_groups=mesh['groups'=2,'ctx'=4,'exp'=2,'tp'=2] {'ctx'}, dimensions={1}, use_global_device_ids=true | all-gather | bytes 2560 | tf_op jit(solution)/shard_map/all_gather | solution.py:81
  19.5 0.7 broadcast_in_dim.55
  20.2 0.2 eq.50
  20.6 1.1 fusion.10
  21.6 2.0 %copy.17 = bf16[128,2,5,128]{3,1,2,0:T(2,128)(2,1)} copy(bf16[128,2,5,128]{3,0,2,1:T(8,128)(2,1)} %bitcast.76) | data formatting | bytes 655360 | tf_op jit(solution)/shard_map/reshape;squeeze | solution.py:34
  23.6 0.8 copy.19
  24.5 2.1 %collective-permute-done.1 = bf16[1,128,2,128]{3,2,1,0:T(2,128)(2,1)S(1)} collective-permute-done((bf16[1,128,2,128]{3,2,1,0:T(2,128)(2,1)S(1)}, bf16[1,128,2,128]{3,2,1,0:T(2,128)(2,1)S(1)}, u32[]{:S(2)}, u32[]{:S(2)}) %collective-permute-start.1) | collective-permute-done | bytes 65568 | tf_op jit(solution)/shard_map/ppermute | solution.py:76
  26.6 14.4 %all_gather.13 = bf16[1,512,2,128]{3,1,2,0:T(8,128)(2,1)S(1)} all-gather(bf16[1,128,2,128]{3,1,2,0:T(8,128)(2,1)S(1)} %copy.19), channel_id=1, replica_groups=mesh['groups'=2,'ctx'=4,'exp'=2,'tp'=2] {'ctx'}, dimensions={1}, use_global_device_ids=true | all-gather | bytes 327680 | tf_op jit(solution)/shard_map/all_gather | solution.py:80
  41.4 0.2 constant_dynamic-slice_fusion
  41.7 0.7 fusion
  42.4 0.6 fusion.3
  43.0 1.2 fusion.21
  44.2 0.3 copy.21
  44.6 0.9 copy.22
  45.5 2.1 %reshape.135 = bf16[2,64,1280]{2,1,0:T(8,128)(2,1)} reshape(bf16[128,2,5,128]{3,2,1,0:T(8,128)(2,1)} %copy.22) | data formatting | bytes 655360 | tf_op jit(solution)/shard_map/reshape | solution.py:97
  47.7 33.9 %all-gather.2.cloned.1.call-done = bf16[2,256,1280]{2,1,0:T(8,128)(2,1)} async-done(((bf16[2,64,1280]{2,1,0:T(8,128)(2,1)}), bf16[2,256,1280]{2,1,0:T(8,128)(2,1)}) %all-gather.2.cloned.1.call-update) | async-done | bytes 1310736 | tf_op jit(solution)/shard_map/all_gather | solution.py:99
  81.6 4.2 %convolution_convert_fusion.1 = bf16[512,1280]{1,0:T(8,128)(2,1)} fusion(bf16[512,1280]{1,0:T(8,128)(2,1)} %bitcast.82, bf16[1280,1280]{1,0:T(8,128)(2,1)S(1)} %copy-done), kind=kOutput, calls=%fused_computation.1 | convolution fusion | flops 1678376960 | bytes 5898240 | tf_op jit(solution)/shard_map/dot_general | solution.py:102
  85.9 7.9 %reduce-scatter.2.cloned.1.call-done = bf16[256,1280]{1,0:T(8,128)(2,1)} async-done(((bf16[512,1280]{1,0:T(8,128)(2,1)}), bf16[256,1280]{1,0:T(8,128)(2,1)}) %reduce-scatter.2.cloned.1.call-update) | async-done | bytes 655376 | tf_op jit(solution)/shard_map/reduce_scatter | solution.py:101
  93.8 5.0 %all-to-all-start = ((bf16[4,64,1280]{2,1,0:T(8,128)(2,1)}), bf16[4,64,1280]{2,1,0:T(8,128)(2,1)}, u32[]{:S(2)}, u32[]{:S(2)}) async-start(bf16[4,64,1280]{2,1,0:T(8,128)(2,1)} %bitcast.75), calls=%async_computation.1 | async-start | bytes 1310720 | tf_op jit(solution)/shard_map/all_to_all | solution.py:109
  98.8 0.2 fusion.17
  99.1 17.4 %all-to-all-done = bf16[4,64,1280]{2,1,0:T(8,128)(2,1)} async-done(((bf16[4,64,1280]{2,1,0:T(8,128)(2,1)}), bf16[4,64,1280]{2,1,0:T(8,128)(2,1)}, u32[]{:S(2)}, u32[]{:S(2)}) %all-to-all-start) | async-done | bytes 655392 | tf_op jit(solution)/shard_map/all_to_all | solution.py:109
  116.5 1.2 convert_bitcast_fusion
  117.7 0.8 copy.23
  118.6 0.2 copy.28
  118.8 0.8 copy-done.1
  119.7 0.3 multiply_reduce_fusion
  120.0 1.6 convolution_convert_fusion
  121.6 3.8 %reshape.137 = bf16[2,32,2,5120]{3,2,1,0:T(2,128)(2,1)} reshape(bf16[128,5120]{1,0:T(8,128)(2,1)} %convolution_convert_fusion) | data formatting | bytes 2621440 | tf_op jit(solution)/shard_map/reshape | solution.py:142
  125.4 19.7 %all_to_all.14 = bf16[2,32,2,5120]{3,2,1,0:T(2,128)(2,1)S(1)} all-to-all(bf16[2,32,2,5120]{3,2,1,0:T(2,128)(2,1)} %reshape.137), channel_id=1, replica_groups=mesh['groups'=2,'ctx'=4,'exp'=2,'tp'=2] {'exp'}, dimensions={0} | all-to-all | bytes 2621440 | tf_op jit(solution)/shard_map/all_to_all | solution.py:143
  145.1 11.5 %fusion.12 = f32[32,1,2,2]{3,1,2,0:T(1,128)S(1)} fusion(bf16[2,32,2,5120]{3,2,1,0:T(2,128)(2,1)S(1)} %all_to_all.14, bf16[5120,32,1,1]{0,1,2,3:T(8,128)(2,1)S(1)} %bitcast.83), kind=kOutput, calls=%fused_computation.21 | convolution fusion | flops 1310720 | bytes 1638912 | tf_op jit(solution)/shard_map/secd,de->sec/dot_general | solution.py:144
  156.8 2.2 %multiply_convert_fusion = bf16[2,32,2,5120]{3,2,1,0:T(2,128)(2,1)} fusion(bf16[2,32,2,5120]{3,2,1,0:T(2,128)(2,1)S(1)} %all_to_all.14, f32[2,32,2]{2,1,0:T(8,128)S(1)} %fusion.38), kind=kLoop, calls=%fused_computation.7 | loop fusion | flops 1966080 | bytes 2621952 | tf_op jit(solution)/shard_map/convert_element_type | solution.py:145
  (43 shorter events, 0.9 us)
Async XLA Ops:
  6.5 75.1 %copy-start = (bf16[1280,1280]{1,0:T(8,128)(2,1)S(1)}, bf16[1280,1280]{1,0:T(8,128)(2,1)}, u32[]{:S(2)}) copy-start(bf16[1280,1280]{1,0:T(8,128)(2,1)} %param.15) | copy-start | bytes 9830404
  6.5 34.6 %copy-start.4 = (bf16[1,128,2,128]{3,2,1,0:T(2,128)(2,1)S(1)}, bf16[1,128,2,128]{3,2,1,0:T(2,128)(2,1)}, u32[]{:S(2)}) copy-start(bf16[1,128,2,128]{3,2,1,0:T(2,128)(2,1)} %param.11) | copy-start | bytes 196612
  6.5 75.1 %all-gather.2.cloned.1.call-start = ((), (), s32[]{:S(2)}) async-start(), calls=%async_computation.3 | async-start | bytes 1638400 | tf_op jit(solution)/shard_map/all_gather | solution.py:99
  6.5 13.9 %collective-permute-start = (bf16[1,128,2,128]{3,2,1,0:T(2,128)(2,1)}, bf16[1,128,2,128]{3,2,1,0:T(2,128)(2,1)S(1)}, u32[]{:S(2)}, u32[]{:S(2)}) collective-permute-start(bf16[1,128,2,128]{3,2,1,0:T(2,128)(2,1)} %param.11), channel_id=1, source_target_pairs={{0,4},{4,8},{8,12},{12,0},{1,5},{5,9},{9,13},{13,1},{2,6},{6,10},{... | collective-permute-start | bytes 196616 | tf_op jit(solution)/shard_map/ppermute | solution.py:76
  20.5 6.1 %collective-permute-start.1 = (bf16[1,128,2,128]{3,2,1,0:T(2,128)(2,1)S(1)}, bf16[1,128,2,128]{3,2,1,0:T(2,128)(2,1)S(1)}, u32[]{:S(2)}, u32[]{:S(2)}) collective-permute-start(bf16[1,128,2,128]{3,2,1,0:T(2,128)(2,1)S(1)} %collective-permute-done), channel_id=1, source_target_pairs={{0,4},{4,8},{8,12},{12,0},{1,5},{5,9},{9,13},{13,1},{2,6},{6,10},{... | collective-permute-start | bytes 196616 | tf_op jit(solution)/shard_map/ppermute | solution.py:76
  24.5 17.1 %copy-start.2 = (pred[640,512]{0,1:T(8,128)(4,1)S(1)}, pred[640,512]{0,1:T(8,128)(4,1)}, u32[]{:S(2)}) copy-start(pred[640,512]{0,1:T(8,128)(4,1)} %fusion.10) | copy-start | bytes 983044
  24.5 17.1 %copy-start.3 = (bf16[128,2,5,128]{3,1,2,0:T(2,128)(2,1)S(1)}, bf16[128,2,5,128]{3,1,2,0:T(2,128)(2,1)}, u32[]{:S(2)}) copy-start(bf16[128,2,5,128]{3,1,2,0:T(2,128)(2,1)} %copy.17) | copy-start | bytes 983044
  26.6 14.4 %collective-permute-start.2 = (bf16[1,128,2,128]{3,2,1,0:T(2,128)(2,1)S(1)}, bf16[1,128,2,128]{3,2,1,0:T(2,128)(2,1)S(1)}, u32[]{:S(2)}, u32[]{:S(2)}) collective-permute-start(bf16[1,128,2,128]{3,2,1,0:T(2,128)(2,1)S(1)} %collective-permute-done.1), channel_id=1, source_target_pairs={{0,4},{4,8},{8,12},{12,0},{1,5},{5,9},{9,13},{13,1},{2,6},{6,10},{... | collective-permute-start | bytes 196616 | tf_op jit(solution)/shard_map/ppermute | solution.py:76
  47.6 46.2 %reduce-scatter.2.cloned.1.call-start = ((), (), s32[]{:S(2)}) async-start(), calls=%async_computation.4 | async-start | bytes 1966080 | tf_op jit(solution)/shard_map/reduce_scatter | solution.py:101
  85.9 13.0 %copy-start.8 = (s32[64]{0:T(128)S(1)}, s32[64]{0:T(128)}, u32[]{:S(2)}) copy-start(s32[64]{0:T(128)} %param.19) | copy-start | bytes 772
  85.9 13.0 %copy-start.5 = (bf16[5120]{0:T(1024)(128)(2,1)S(1)}, bf16[5120]{0:T(1024)(128)(2,1)}, u32[]{:S(2)}) copy-start(bf16[5120]{0:T(1024)(128)(2,1)} %param.16) | copy-start | bytes 30724
  85.9 13.0 %copy-start.6 = (s32[1,64,1]{1,2,0:T(1,128)S(1)}, s32[1,64,1]{1,2,0:T(1,128)}, u32[]{:S(2)}) copy-start(s32[1,64,1]{1,2,0:T(1,128)} %param.18) | copy-start | bytes 772
  93.8 22.7 %all-to-all-start = ((bf16[4,64,1280]{2,1,0:T(8,128)(2,1)}), bf16[4,64,1280]{2,1,0:T(8,128)(2,1)}, u32[]{:S(2)}, u32[]{:S(2)}) async-start(bf16[4,64,1280]{2,1,0:T(8,128)(2,1)} %bitcast.75), calls=%async_computation.1 | async-start | bytes 1310720 | tf_op jit(solution)/shard_map/all_to_all | solution.py:109
  118.6 1.1 copy-start.1
  125.4 19.7 %copy-start.7 = (bf16[5120,32]{0,1:T(8,128)(2,1)S(1)}, bf16[5120,32]{0,1:T(8,128)(2,1)}, u32[]{:S(2)}) copy-start(bf16[5120,32]{0,1:T(8,128)(2,1)} %param.17) | copy-start | bytes 983044
Sparse Core Ops, SparseCore 0:
  47.7 33.8 all-gather.1
  86.0 7.7 reduce-scatter.1
